TPU v7x, 256 devices: a whole 4x4x8 slice. The times are simulated.
256 devices in a mesh: dp: 4 (over x), expert: 64 (over z, y, core).
Axes of the slice: x: 4, y: 4, z: 8, core: 2. Of those that a mesh axis runs over, the one named last changes fastest.
Arguments:
- tokens: bfloat16 [4096, 3584], P('expert'), may hold values from -6 to 6
- expert_ids: int32 [4096, 8], P('expert'), may hold values from 0 to 63, all different within a row; in each aligned block of 64 rows (0 to 63, 64 to 127, ...) at most 8 rows name the same one
- weight_num: int32 [4096, 8], P('expert'), may hold values from 64 to 1023
- gate_proj: bfloat16 [64, 3584, 2048], P('expert', None, 'dp'), may hold values from -0.09375 to 0.09375
- up_proj: bfloat16 [64, 3584, 2048], P('expert', None, 'dp'), may hold values from -0.09375 to 0.09375
- down_proj: bfloat16 [64, 2048, 3584], P('expert', 'dp'), may hold values from -0.125 to 0.125
Outputs:
- combined: bfloat16 [4096, 3584], P('expert', 'dp')
Inputs may be any that keep to these rules, and one draw needn't show every extreme that they name: `expert_ids`: in the 64 rows of one device no expert is named by more than 8 rows, and some device has an expert named by exactly 8 of its rows.
All inputs are finite; a program needn't handle non-finite values.
Results may differ from a plain program's by a relative error of at most 0.015.
Values may be sent and summed in bfloat16 or wider, within the bound.
A program may use at most 192 MiB of HBM per device.

v0:
```python
import jax
import jax.numpy as jnp
from jax import lax
from jax.sharding import PartitionSpec as P

ROOM = 8


def slot_matrices(ids, num, experts, capacity):
    rows = ids.shape[0]
    slots = experts * capacity
    column = jnp.arange(slots, dtype=jnp.int32)[None, :]
    expert_of = column // capacity
    hits = [ids[:, k : k + 1] == expert_of for k in range(ids.shape[1])]
    named = sum((h.astype(jnp.float32) for h in hits))
    weight = sum((jnp.where(h, num[:, k : k + 1], 0) for k, h in enumerate(hits)))
    earlier = jnp.arange(rows)[:, None] > jnp.arange(rows)[None, :]
    position = jnp.dot(
        earlier.astype(jnp.bfloat16), named.astype(jnp.bfloat16), preferred_element_type=jnp.float32
    )
    here = (named > 0) & (position == (column % capacity).astype(jnp.float32))
    high = jnp.where(here, weight // 32 * 32, 0).astype(jnp.bfloat16)
    low = jnp.where(here, weight % 32, 0).astype(jnp.bfloat16)
    return (here.astype(jnp.bfloat16), high, low)


def local(tokens, expert_ids, weight_num, gate_proj, up_proj, down_proj):
    experts = lax.axis_size("expert")
    parts = lax.axis_size("dp")
    width = tokens.shape[1]
    quarter = width // parts
    slots = experts * ROOM
    here, high, low = slot_matrices(expert_ids, weight_num, experts, ROOM)
    mine = lax.dynamic_slice_in_dim(tokens, lax.axis_index("dp") * quarter, quarter, 1)
    outgoing = lax.dot_general(
        here, mine, (((0,), (0,)), ((), ())), preferred_element_type=jnp.float32
    ).astype(jnp.bfloat16)
    arrived = lax.all_to_all(
        outgoing.reshape(experts, ROOM, quarter), "expert", split_axis=0, concat_axis=0, tiled=True
    ).reshape(slots, quarter)
    rows = lax.all_gather(arrived, "dp", axis=0, tiled=True)
    gate_out, up_out = (0.0, 0.0)
    for q in range(parts):
        block = rows[q * slots : (q + 1) * slots]
        cut = slice(q * quarter, (q + 1) * quarter)
        gate_out += jnp.dot(block, gate_proj[0, cut], preferred_element_type=jnp.float32)
        up_out += jnp.dot(block, up_proj[0, cut], preferred_element_type=jnp.float32)
    hidden = (jax.nn.silu(gate_out) * up_out).astype(jnp.bfloat16)
    partial = jnp.concatenate(
        [
            jnp.dot(
                hidden,
                down_proj[0, :, q * quarter : (q + 1) * quarter],
                preferred_element_type=jnp.float32,
            ).astype(jnp.bfloat16)
            for q in range(parts)
        ],
        axis=0,
    )
    summed = lax.psum_scatter(partial, "dp", scatter_dimension=0, tiled=True)
    returned = lax.all_to_all(
        summed.reshape(experts, ROOM, quarter), "expert", split_axis=0, concat_axis=0, tiled=True
    ).reshape(slots, quarter)
    total = jnp.dot(high, returned, preferred_element_type=jnp.float32)
    total += jnp.dot(low, returned, preferred_element_type=jnp.float32)
    return (total / 1024.0).astype(jnp.bfloat16)


def solution(mesh):
    placed = (
        P("expert", None),
        P("expert", None),
        P("expert", None),
        P("expert", None, "dp"),
        P("expert", None, "dp"),
        P("expert", "dp", None),
    )
    return jax.shard_map(
        local, mesh=mesh, in_specs=placed, out_specs=P("expert", "dp"), check_vma=False
    )
```

profile of v0, /device:TPU:1, one launch (start us, length us, event | category | flops | bytes accessed | tf_op | source)
XLA Modules:
  0.0 203.0 jit_solution(10615380470221626891)
XLA Ops:
  6.5 0.0 copy-start
  6.5 0.0 all-gather.2.cloned.1.call-start
  6.5 1.0 slice_bitcast_fusion.15
  7.5 0.3 fusion.5
  7.9 0.0 copy-done
  7.9 0.5 fusion.1
  8.3 38.4 %all_to_all.10 = bf16[64,8,896]{2,1,0:T(8,128)(2,1)} all-to-all(bf16[64,8,896]{2,1,0:T(8,128)(2,1)S(1)} %fusion.1), channel_id=1, replica_groups=mesh['dp'=4,'expert'=64] {'expert'}, dimensions={0} | all-to-all | bytes 1835008 | tf_op jit(solution)/shard_map/all_to_all | solution.py:38
  46.7 0.0 all-gather.2.cloned.1.call-update
  46.7 0.0 reduce-scatter.2.cloned.1.call-start
  46.8 43.6 %all-gather.2.cloned.1.call-done = bf16[2048,896]{1,0:T(8,128)(2,1)} async-done(((bf16[512,896]{1,0:T(8,128)(2,1)}), bf16[2048,896]{1,0:T(8,128)(2,1)}) %all-gather.2.cloned.1.call-update) | async-done | bytes 3670032 | tf_op jit(solution)/shard_map/all_gather | solution.py:41
  90.4 0.0 copy-start.1
  90.4 0.0 copy-start.2
  90.4 2.3 %fusion.21 = f32[512,512]{1,0:T(8,128)S(1)} fusion(bf16[1,3584,512]{2,1,0:T(8,128)(2,1)} %param.9, bf16[2048,896]{1,0:T(8,128)(2,1)} %all-gather.2.cloned.1.call-done), kind=kOutput, calls=%fused_computation.35 | convolution fusion | flops 469762048 | bytes 2883584 | tf_op jit(solution)/shard_map/dot_general | solution.py:46
  92.7 2.5 %convolution_add_fusion.5 = f32[512,512]{1,0:T(8,128)S(1)} fusion(f32[512,512]{1,0:T(8,128)S(1)} %fusion.21, bf16[1,3584,512]{2,1,0:T(8,128)(2,1)} %param.9, bf16[2048,896]{1,0:T(8,128)(2,1)} %all-gather.2.cloned.1.call-done), kind=kOutput, calls=%fused_computation.12 | convolution fusion | flops 470024192 | bytes 3932160 | tf_op jit(solution)/shard_map/dot_general | solution.py:46
  95.3 0.0 copy-done.1
  95.3 0.0 copy-done.2
  95.3 0.0 copy-start.3
  95.3 0.7 convolution_add_fusion.4
  96.0 0.7 convolution_add_fusion.3
  96.7 0.6 copy-done.3
  97.3 0.7 fusion.16
  98.0 0.7 convolution_add_fusion.2
  98.7 0.7 convolution_add_fusion.1
  99.5 0.0 copy-start.5
  99.5 0.8 fusion.2
  100.3 1.2 copy-done.5
  101.5 0.7 convolution_convert_fusion.1
  102.2 0.7 convolution_convert_fusion.2
  102.9 0.7 convolution_convert_fusion.3
  103.7 0.7 convolution_convert_fusion.4
  104.4 8.7 %pad_maximum_fusion = bf16[2048,896]{1,0:T(8,128)(2,1)} fusion(bf16[512,896]{1,0:T(8,128)(2,1)S(1)} %convolution_convert_fusion.1, bf16[512,896]{1,0:T(8,128)(2,1)S(1)} %convolution_convert_fusion.2, bf16[512,896]{1,0:T(8,128)(2,1)S(1)} %convolution_convert_fusion.3, bf16[512,896]{1,0:T(8,128)(2,1)S(1)} %convolution_convert_fusion.4), kind=kLoop, calls=%fused_computation | loop fusion | flops 14680064 | bytes 7340032 | tf_op jit(solution)/shard_map/concatenate | solution.py:49
  113.1 0.0 copy-start.4
  113.1 0.0 reduce-scatter.2.cloned.1.call-update
  113.1 45.6 %reduce-scatter.2.cloned.1.call-done = bf16[512,896]{1,0:T(8,128)(2,1)} async-done(((bf16[2048,896]{1,0:T(8,128)(2,1)}), bf16[512,896]{1,0:T(8,128)(2,1)}) %reduce-scatter.2.cloned.1.call-update) | async-done | bytes 917520 | tf_op jit(solution)/shard_map/reduce_scatter | solution.py:60
  158.7 10.6 %all-to-all-start.1 = ((bf16[64,8,896]{2,1,0:T(8,128)(2,1)}), bf16[64,8,896]{2,1,0:T(8,128)(2,1)S(1)}, u32[]{:S(2)}, u32[]{:S(2)}) async-start(bf16[64,8,896]{2,1,0:T(8,128)(2,1)} %bitcast.83), calls=%async_computation.2 | async-start | bytes 1835008 | tf_op jit(solution)/shard_map/all_to_all | solution.py:61
  169.3 0.0 copy-done.4
  169.4 25.3 %all-to-all-done.1 = bf16[64,8,896]{2,1,0:T(8,128)(2,1)S(1)} async-done(((bf16[64,8,896]{2,1,0:T(8,128)(2,1)}), bf16[64,8,896]{2,1,0:T(8,128)(2,1)S(1)}, u32[]{:S(2)}, u32[]{:S(2)}) %all-to-all-start.1) | async-done | bytes 917536 | tf_op jit(solution)/shard_map/all_to_all | solution.py:61
  194.6 0.5 fusion.7
  195.1 1.1 fusion.4
  (2 shorter events, 0.0 us)
Async XLA Ops:
  6.5 1.3 copy-start
  6.5 83.9 %all-gather.2.cloned.1.call-start = ((), (), s32[]{:S(2)}) async-start(), calls=%async_computation.3 | async-start | bytes 4587520 | tf_op jit(solution)/shard_map/all_gather | solution.py:41
  46.7 112.0 %reduce-scatter.2.cloned.1.call-start = ((), (), s32[]{:S(2)}) async-start(), calls=%async_computation.4 | async-start | bytes 4587520 | tf_op jit(solution)/shard_map/reduce_scatter | solution.py:60
  90.4 4.9 %copy-start.1 = (bf16[2048,896]{1,0:T(8,128)(2,1)S(1)}, bf16[2048,896]{1,0:T(8,128)(2,1)}, u32[]{:S(2)}) copy-start(bf16[2048,896]{1,0:T(8,128)(2,1)} %all-gather.2.cloned.1.call-done) | copy-start | bytes 11010052
  90.4 4.9 %copy-start.2 = (bf16[1,3584,512]{2,1,0:T(8,128)(2,1)S(1)}, bf16[1,3584,512]{2,1,0:T(8,128)(2,1)}, u32[]{:S(2)}) copy-start(bf16[1,3584,512]{2,1,0:T(8,128)(2,1)} %param.9) | copy-start | bytes 11010052
  95.3 2.0 %copy-start.3 = (bf16[1,3584,512]{2,1,0:T(8,128)(2,1)S(1)}, bf16[1,3584,512]{2,1,0:T(8,128)(2,1)}, u32[]{:S(2)}) copy-start(bf16[1,3584,512]{2,1,0:T(8,128)(2,1)} %param.10) | copy-start | bytes 11010052
  99.5 2.0 %copy-start.5 = (bf16[1,512,3584]{2,1,0:T(8,128)(2,1)S(1)}, bf16[1,512,3584]{2,1,0:T(8,128)(2,1)}, u32[]{:S(2)}) copy-start(bf16[1,512,3584]{2,1,0:T(8,128)(2,1)} %param.11) | copy-start | bytes 11010052
  113.1 56.2 %copy-start.4 = (s32[64,8]{0,1:T(8,128)S(1)}, s32[64,8]{0,1:T(8,128)}, u32[]{:S(2)}) copy-start(s32[64,8]{0,1:T(8,128)} %param.8) | copy-start | bytes 6148
  158.7 35.9 %all-to-all-start.1 = ((bf16[64,8,896]{2,1,0:T(8,128)(2,1)}), bf16[64,8,896]{2,1,0:T(8,128)(2,1)S(1)}, u32[]{:S(2)}, u32[]{:S(2)}) async-start(bf16[64,8,896]{2,1,0:T(8,128)(2,1)} %bitcast.83), calls=%async_computation.2 | async-start | bytes 1835008 | tf_op jit(solution)/shard_map/all_to_all | solution.py:61
Sparse Core Ops, SparseCore 0:
  46.8 43.5 all-gather.1
  113.2 45.3 reduce-scatter.1
where the time goes:
time: 203 us
  waiting for transfers between devices  115 us (57%)
  blocking collectives  38.4 us (19%)
  matrix products  14.4 us (7%)
  between operations  13.6 us (7%)
  starting transfers between devices  10.7 us (5%)
  other arithmetic  8.73 us (4%)
  local copies, waits for them, and re-layouts  2.81 us (1%)
    reduce_scatter x1, waiting for transfers between devices, local(): summed = lax.psum_scatter(partial, 'dp', scatter_dimension=0, tiled=True)  45.6 us
    all_gather x1, waiting for transfers between devices, local(): rows = lax.all_gather(arrived, 'dp', axis=0, tiled=True)  43.6 us
    all_to_all x1, blocking collectives, local(): lax.all_to_all(outgoing.reshape(experts, ROOM, quarter), 'expert', split_...  38.4 us
    all_to_all x1, waiting for transfers between devices, local(): lax.all_to_all(summed.reshape(experts, ROOM, quarter), 'expert', split_ax...  25.3 us
    all_to_all x1, starting transfers between devices, local(): lax.all_to_all(summed.reshape(experts, ROOM, quarter), 'expert', split_ax...  10.6 us
    concatenate x1, other arithmetic, local(): jnp.concatenate([jnp.dot(hidden, down_proj[0, :, q * quarter:(q + 1) * qu...  8.72 us
    dot_general x4, matrix products, local(): jnp.dot(block, gate_proj[0, cut], preferred_element_type=jnp.float32)  6.26 us
  transfers between devices with their start and end apart: 3, of which 3 were waited for; matrix products, arithmetic and copies ran while one was open for 0% of the time, Pallas kernels for 0%

commit v1 on v0

--- a/solution.py
+++ b/solution.py
@@ -38,7 +38,9 @@
     arrived = lax.all_to_all(
         outgoing.reshape(experts, ROOM, quarter), "expert", split_axis=0, concat_axis=0, tiled=True
     ).reshape(slots, quarter)
-    rows = lax.all_gather(arrived, "dp", axis=0, tiled=True)
+    rows = jnp.concatenate(
+        lax.all_to_all(jnp.stack([arrived] * lax.axis_size("dp")), "dp", 0, 0), axis=0
+    )
     gate_out, up_out = (0.0, 0.0)
     for q in range(parts):
         block = rows[q * slots : (q + 1) * slots]

time: 203 us -> 199 us (0.980)
  waiting for transfers between devices: 115 us -> 67.5 us
  blocking collectives: 38.4 us -> 83.9 us
  matrix products: 14.4 us -> 10.9 us
    all_to_all x0 -> x1, blocking collectives: none -> 45.6 us  [local(): lax.all_to_all(jnp.stack([arrived] * lax.axis_size('dp')), 'dp', 0, 0)]
    all_gather x1 -> x0, waiting for transfers between devices: 43.6 us -> none  [local(): rows = lax.all_gather(arrived, 'dp', axis=0, tiled=True)]
    dot_general x4, matrix products: 6.26 us -> 2.82 us  [local(): jnp.dot(block, gate_proj[0, cut], preferred_element_type=jnp.float32)]
    reduce_scatter x1, waiting for transfers between devices: 45.6 us -> 42.2 us  [local(): summed = lax.psum_scatter(partial, 'dp', scatter_dimension=0, tiled=True)]
  transfers between devices with their start and end apart: 3 -> 2, of which waited for: 3 -> 2; matrix products, arithmetic and copies ran while one was open for 0% -> 0% of each run, Pallas kernels for 0% -> 0%
where the time goes in v1:
time: 199 us; the launch traced here: 198 us
  blocking collectives  83.9 us (42%)
  waiting for transfers between devices  67.5 us (34%)
  between operations  13.6 us (7%)
  matrix products  10.9 us (5%)
  starting transfers between devices  10.6 us (5%)
  other arithmetic  8.73 us (4%)
  local copies, waits for them, and re-layouts  3.08 us (2%)
    all_to_all x1, blocking collectives, local(): lax.all_to_all(jnp.stack([arrived] * lax.axis_size('dp')), 'dp', 0, 0)  45.6 us
    reduce_scatter x1, waiting for transfers between devices, local(): summed = lax.psum_scatter(partial, 'dp', scatter_dimension=0, tiled=True)  42.2 us
    all_to_all x1, blocking collectives, local(): lax.all_to_all(outgoing.reshape(experts, ROOM, quarter), 'expert', split_...  38.3 us
    all_to_all x1, waiting for transfers between devices, local(): lax.all_to_all(summed.reshape(experts, ROOM, quarter), 'expert', split_ax...  25.3 us
    all_to_all x1, starting transfers between devices, local(): lax.all_to_all(summed.reshape(experts, ROOM, quarter), 'expert', split_ax...  10.6 us
    concatenate x1, other arithmetic, local(): jnp.concatenate([jnp.dot(hidden, down_proj[0, :, q * quarter:(q + 1) * qu...  8.73 us
  transfers between devices with their start and end apart: 2, of which 2 were waited for; matrix products, arithmetic and copies ran while one was open for 0% of the time, Pallas kernels for 0%

profile of v1, /device:TPU:1, one launch (start us, length us, event | category | flops | bytes accessed | tf_op | source)
XLA Modules:
  0.0 198.3 jit_solution(8852733025367053792)
XLA Ops:
  6.5 0.0 copy-start
  6.5 0.0 reduce-scatter.2.cloned.1.call-start
  6.5 1.0 slice_bitcast_fusion.27
  7.5 0.3 fusion.5
  7.9 0.0 copy-done
  7.9 0.5 fusion.1
  8.3 38.3 %all_to_all.15 = bf16[64,8,896]{2,1,0:T(8,128)(2,1)S(1)} all-to-all(bf16[64,8,896]{2,1,0:T(8,128)(2,1)S(1)} %fusion.1), channel_id=1, replica_groups=mesh['dp'=4,'expert'=64] {'expert'}, dimensions={0} | all-to-all | bytes 1835008 | tf_op jit(solution)/shard_map/all_to_all | solution.py:38
  46.6 0.3 stack.3
  46.9 0.0 copy-start.1
  46.9 45.6 %all_to_all.16 = bf16[4,512,896]{2,1,0:T(8,128)(2,1)S(1)} all-to-all(bf16[4,512,896]{2,1,0:T(8,128)(2,1)S(1)} %stack.3), channel_id=1, replica_groups=mesh['dp'=4,'expert'=64] {'dp'}, dimensions={0} | all-to-all | bytes 7340032 | tf_op jit(solution)/shard_map/all_to_all | solution.py:42
  92.5 0.0 copy-done.1
  92.5 0.7 fusion.21
  93.2 0.7 convolution_add_fusion.5
  93.9 0.0 copy-start.2
  94.0 0.7 convolution_add_fusion.4
  94.7 0.7 convolution_add_fusion.3
  95.4 0.6 copy-done.2
  96.0 0.7 fusion.16
  96.7 0.7 convolution_add_fusion.2
  97.4 0.7 convolution_add_fusion.1
  98.1 0.0 copy-start.4
  98.1 0.8 fusion.2
  99.0 1.2 copy-done.4
  100.2 0.7 convolution_convert_fusion.1
  100.9 0.7 convolution_convert_fusion.2
  101.6 0.7 convolution_convert_fusion.3
  102.3 0.7 convolution_convert_fusion.4
  103.0 8.7 %pad_maximum_fusion = bf16[2048,896]{1,0:T(8,128)(2,1)} fusion(bf16[512,896]{1,0:T(8,128)(2,1)S(1)} %convolution_convert_fusion.1, bf16[512,896]{1,0:T(8,128)(2,1)S(1)} %convolution_convert_fusion.2, bf16[512,896]{1,0:T(8,128)(2,1)S(1)} %convolution_convert_fusion.3, bf16[512,896]{1,0:T(8,128)(2,1)S(1)} %convolution_convert_fusion.4), kind=kLoop, calls=%fused_computation | loop fusion | flops 14680064 | bytes 7340032 | tf_op jit(solution)/shard_map/concatenate | solution.py:51
  111.7 0.0 copy-start.3
  111.7 0.0 reduce-scatter.2.cloned.1.call-update
  111.8 42.2 %reduce-scatter.2.cloned.1.call-done = bf16[512,896]{1,0:T(8,128)(2,1)} async-done(((bf16[2048,896]{1,0:T(8,128)(2,1)}), bf16[512,896]{1,0:T(8,128)(2,1)}) %reduce-scatter.2.cloned.1.call-update) | async-done | bytes 917520 | tf_op jit(solution)/shard_map/reduce_scatter | solution.py:62
  154.0 10.6 %all-to-all-start.2 = ((bf16[64,8,896]{2,1,0:T(8,128)(2,1)}), bf16[64,8,896]{2,1,0:T(8,128)(2,1)S(1)}, u32[]{:S(2)}, u32[]{:S(2)}) async-start(bf16[64,8,896]{2,1,0:T(8,128)(2,1)} %bitcast.99), calls=%async_computation.3 | async-start | bytes 1835008 | tf_op jit(solution)/shard_map/all_to_all | solution.py:63
  164.6 0.0 copy-done.3
  164.6 25.3 %all-to-all-done.2 = bf16[64,8,896]{2,1,0:T(8,128)(2,1)S(1)} async-done(((bf16[64,8,896]{2,1,0:T(8,128)(2,1)}), bf16[64,8,896]{2,1,0:T(8,128)(2,1)S(1)}, u32[]{:S(2)}, u32[]{:S(2)}) %all-to-all-start.2) | async-done | bytes 917536 | tf_op jit(solution)/shard_map/all_to_all | solution.py:63
  189.9 0.5 fusion.7
  190.4 1.1 fusion.4
  (2 shorter events, 0.0 us)
Async XLA Ops:
  6.5 1.3 copy-start
  6.5 147.4 %reduce-scatter.2.cloned.1.call-start = ((), (), s32[]{:S(2)}) async-start(), calls=%async_computation.4 | async-start | bytes 4587520 | tf_op jit(solution)/shard_map/reduce_scatter | solution.py:62
  46.9 45.7 %copy-start.1 = (bf16[1,3584,512]{2,1,0:T(8,128)(2,1)S(1)}, bf16[1,3584,512]{2,1,0:T(8,128)(2,1)}, u32[]{:S(2)}) copy-start(bf16[1,3584,512]{2,1,0:T(8,128)(2,1)} %param.9) | copy-start | bytes 11010052
  93.9 2.0 %copy-start.2 = (bf16[1,3584,512]{2,1,0:T(8,128)(2,1)S(1)}, bf16[1,3584,512]{2,1,0:T(8,128)(2,1)}, u32[]{:S(2)}) copy-start(bf16[1,3584,512]{2,1,0:T(8,128)(2,1)} %param.10) | copy-start | bytes 11010052
  98.1 2.0 %copy-start.4 = (bf16[1,512,3584]{2,1,0:T(8,128)(2,1)S(1)}, bf16[1,512,3584]{2,1,0:T(8,128)(2,1)}, u32[]{:S(2)}) copy-start(bf16[1,512,3584]{2,1,0:T(8,128)(2,1)} %param.11) | copy-start | bytes 11010052
  111.7 52.9 %copy-start.3 = (s32[64,8]{0,1:T(8,128)S(1)}, s32[64,8]{0,1:T(8,128)}, u32[]{:S(2)}) copy-start(s32[64,8]{0,1:T(8,128)} %param.8) | copy-start | bytes 6148
  154.0 35.9 %all-to-all-start.2 = ((bf16[64,8,896]{2,1,0:T(8,128)(2,1)}), bf16[64,8,896]{2,1,0:T(8,128)(2,1)S(1)}, u32[]{:S(2)}, u32[]{:S(2)}) async-start(bf16[64,8,896]{2,1,0:T(8,128)(2,1)} %bitcast.99), calls=%async_computation.3 | async-start | bytes 1835008 | tf_op jit(solution)/shard_map/all_to_all | solution.py:63
Sparse Core Ops, SparseCore 0:
  111.9 42.0 reduce-scatter.1
